TPU v7x, 512 devices: a whole 4x4x16 slice. The times are simulated.
512 devices in a mesh: dp: 64 (over z, x_lo, core), head: 8 (over x_hi, y).
Axes of the slice: x: 4 (x_hi: 2, x_lo: 2; x = x_hi * 2 + x_lo), y: 4, z: 16, core: 2. Of those that a mesh axis runs over, the one named last changes fastest.
Arguments:
- layer_input: bfloat16 [65536, 8192], P('dp', 'head'), may hold values from -0.09375 to 0.09375
- query_states: bfloat16 [65536, 4096], P(('dp', 'head')), may hold values from -7.5 to 7.5
- key_states: bfloat16 [65536, 1024], P(('dp', 'head')), may hold values from -6 to 6
- value_states: bfloat16 [65536, 1024], P(('dp', 'head')), may hold values from -6 to 6
- out_grad: bfloat16 [65536, 4096], P(('dp', 'head')), may hold values from -6 to 6
- parents: int32 [65536], P('dp'), may hold values from 0 to 510, as said below
- lengths: int32 [128], P('dp'), may hold values from 1 to 512, 40960 in all
Outputs:
- weight_gradient: float32 [1024, 8192], P('dp', 'head')
- value_gradient: bfloat16 [65536, 1024], P(('dp', 'head'))
Inputs may be any that keep to these rules, and one draw needn't show every extreme that they name: `parents`: within each tree a token's parent is an earlier token of the same tree; the first token of a tree is its own parent. The lengths of all trees sum to 40960.
All inputs are finite; a program needn't handle non-finite values. No bound on the sum of `lengths` on one device may be relied on, other than what follows from the above.
Results may differ from a plain program's by a relative error of at most 0.0049.
Values may be sent and summed in bfloat16 or wider, within the bound.
No kernel may reach another device: no remote copies, remote signals or barrier semaphores. Data moves between devices by JAX's collectives and lax.ppermute only.
A program may use at most 64 MiB of HBM per device.

v0:
```python
import jax
import jax.numpy as jnp
from jax import lax
from jax.sharding import PartitionSpec as P

HEAD_DIM = 128
TREE_LEN = 512


def ancestry_of(parent_tree):
    slots = parent_tree.shape[0]
    positions = jnp.arange(slots, dtype=jnp.int32)
    reached = positions[:, None] == positions[None, :]
    jumps = parent_tree
    for number in range(max(1, (slots - 1).bit_length())):
        reached = reached | reached[jumps]
        jumps = jumps[jumps]
    return reached


def block_grads(query_part, grad_part, key_heads, value_heads, live_pairs):
    scaling = HEAD_DIM ** (-0.5)
    scores = (
        jnp.einsum("ikgd,jkd->kgij", query_part, key_heads, preferred_element_type=jnp.float32)
        * scaling
    )
    masked = jnp.where(live_pairs, scores, jnp.float32(-1e30))
    maxima = jnp.max(masked, axis=-1, keepdims=True)
    exponent = jnp.where(live_pairs, jnp.exp(masked - maxima), jnp.float32(0.0))
    row_sums = jnp.sum(exponent, axis=-1, keepdims=True)
    softmax_weights = exponent / jnp.maximum(row_sums, 1.0)
    value_scores = jnp.einsum(
        "ikgd,jkd->kgij", grad_part, value_heads, preferred_element_type=jnp.float32
    )
    row_dots = jnp.sum(softmax_weights * value_scores, axis=-1, keepdims=True)
    score_grads = (softmax_weights * (value_scores - row_dots) * scaling).astype(jnp.bfloat16)
    key_part = jnp.einsum(
        "kgij,ikgd->jkd", score_grads, query_part, preferred_element_type=jnp.float32
    )
    value_part = jnp.einsum(
        "kgij,ikgd->jkd",
        softmax_weights.astype(jnp.bfloat16),
        grad_part,
        preferred_element_type=jnp.float32,
    )
    return (key_part, value_part)


def tree_grads(query_tree, grad_tree, key_tree, value_tree, parent_tree, tree_length):
    kv_local = key_tree.shape[1] // HEAD_DIM
    groups = query_tree.shape[1] // key_tree.shape[1]
    query_heads = query_tree.reshape(TREE_LEN, kv_local, groups, HEAD_DIM)
    grad_heads = grad_tree.reshape(TREE_LEN, kv_local, groups, HEAD_DIM)
    key_heads = key_tree.reshape(TREE_LEN, kv_local, HEAD_DIM)
    value_heads = value_tree.reshape(TREE_LEN, kv_local, HEAD_DIM)
    ancestry = ancestry_of(parent_tree)
    positions = jnp.arange(TREE_LEN, dtype=jnp.int32)
    live_pairs = ancestry & (positions < tree_length)[:, None]
    key_sum, value_sum = block_grads(query_heads, grad_heads, key_heads, value_heads, live_pairs)
    return (
        key_sum.astype(jnp.bfloat16).reshape(TREE_LEN, kv_local * HEAD_DIM),
        value_sum.astype(jnp.bfloat16).reshape(TREE_LEN, kv_local * HEAD_DIM),
    )


def local(layer_input, query_states, key_states, value_states, out_grad, parents, lengths):
    queries, grads_out, keys_here, values_here = (
        lax.all_to_all(query_states, "head", split_axis=1, concat_axis=0, tiled=True),
        lax.all_to_all(out_grad, "head", split_axis=1, concat_axis=0, tiled=True),
        lax.all_to_all(key_states, "head", split_axis=1, concat_axis=0, tiled=True),
        lax.all_to_all(value_states, "head", split_axis=1, concat_axis=0, tiled=True),
    )
    trees = lengths.shape[0]
    stacked = (
        queries.reshape(trees, TREE_LEN, -1),
        grads_out.reshape(trees, TREE_LEN, -1),
        keys_here.reshape(trees, TREE_LEN, -1),
        values_here.reshape(trees, TREE_LEN, -1),
        parents.reshape(trees, TREE_LEN),
        lengths,
    )
    key_grads, value_grads = lax.map(lambda items: tree_grads(*items), stacked)
    key_grads = key_grads.reshape(trees * TREE_LEN, -1)
    value_grads = value_grads.reshape(trees * TREE_LEN, -1)
    key_all = lax.all_gather(key_grads, "head", axis=1, tiled=True)
    weight_gradient = lax.psum_scatter(
        lax.dot_general(
            key_all, layer_input, (((0,), (0,)), ((), ())), preferred_element_type=jnp.float32
        ),
        "dp",
        scatter_dimension=0,
        tiled=True,
    )
    value_gradient = lax.all_to_all(value_grads, "head", split_axis=0, concat_axis=1, tiled=True)
    return (weight_gradient, value_gradient)


def solution(mesh):
    placed = (
        P("dp", "head"),
        P(("dp", "head"), None),
        P(("dp", "head"), None),
        P(("dp", "head"), None),
        P(("dp", "head"), None),
        P("dp"),
        P("dp"),
    )
    return jax.shard_map(
        local,
        mesh=mesh,
        in_specs=placed,
        out_specs=(P("dp", "head"), P(("dp", "head"), None)),
        check_vma=False,
    )
```

profile of v0, /device:TPU:8, one launch (start us, length us, event | category | flops | bytes accessed | tf_op | source)
XLA Modules:
  0.0 527.1 jit_solution(8759982383548423130)
XLA Ops:
  7.2 1.8 copy_bitcast_fusion.1
  9.0 9.7 %all-to-all-start.1 = ((bf16[128,8,128]{2,0,1:T(8,128)(2,1)}), bf16[128,8,128]{2,0,1:T(8,128)(2,1)}, u32[]{:S(2)}, u32[]{:S(2)}) async-start(bf16[128,8,128]{2,0,1:T(8,128)(2,1)} %copy_bitcast_fusion.1), calls=%async_computation.1 | async-start | bytes 524288 | tf_op jit(solution)/shard_map/all_to_all | solution.py:70
  18.7 2.3 copy.45
  21.0 4.8 all-to-all-done.1
  25.8 5.3 all-to-all-start
  31.1 2.3 copy.49
  33.4 8.8 %all-to-all-done = bf16[128,8,512]{0,2,1:T(8,128)(2,1)S(1)} async-done(((bf16[128,8,512]{0,2,1:T(8,128)(2,1)}), bf16[128,8,512]{0,2,1:T(8,128)(2,1)S(1)}, u32[]{:S(2)}, u32[]{:S(2)}) %all-to-all-start) | async-done | bytes 1048608 | tf_op jit(solution)/shard_map/all_to_all | solution.py:68
  42.2 5.7 %all-to-all-start.3 = ((bf16[128,8,512]{0,2,1:T(8,128)(2,1)}), bf16[128,8,512]{0,2,1:T(8,128)(2,1)}, u32[]{:S(2)}, u32[]{:S(2)}) async-start(bf16[128,8,512]{0,2,1:T(8,128)(2,1)} %bitcast.261), calls=%async_computation.3 | async-start | bytes 2097152 | tf_op jit(solution)/shard_map/all_to_all | solution.py:69
  48.6 12.5 %all-to-all-done.3 = bf16[128,8,512]{0,2,1:T(8,128)(2,1)} async-done(((bf16[128,8,512]{0,2,1:T(8,128)(2,1)}), bf16[128,8,512]{0,2,1:T(8,128)(2,1)}, u32[]{:S(2)}, u32[]{:S(2)}) %all-to-all-start.3) | async-done | bytes 1048608 | tf_op jit(solution)/shard_map/all_to_all | solution.py:69
  61.1 5.4 %all-to-all-start.2 = ((bf16[128,8,128]{2,0,1:T(8,128)(2,1)}), bf16[128,8,128]{2,0,1:T(8,128)(2,1)}, u32[]{:S(2)}, u32[]{:S(2)}) async-start(bf16[128,8,128]{2,0,1:T(8,128)(2,1)} %copy_bitcast_fusion), calls=%async_computation.2 | async-start | bytes 524288 | tf_op jit(solution)/shard_map/all_to_all | solution.py:71
  68.4 2.3 copy.50
  70.7 2.9 all-to-all-done.2
  73.6 134.2 %while.12 = (s32[]{:T(128)}, bf16[2,512,128]{2,1,0:T(8,128)(2,1)}, bf16[2,512,128]{2,1,0:T(8,128)(2,1)}, bf16[2,512,512]{2,1,0:T(8,128)(2,1)}, s32[2,512]{1,0:T(...) while((s32[]{:T(128)}, bf16[2,512,128]{2,1,0:T(8,128)(2,1)}, ...), condition=%wide.region_4.5_spmd, body=%wide.region_0.4_spmd.sunk | while | flops 1109019648 | bytes 93070192 | solution.py:82
  74.3 3.5 gather_fusion.1
  79.8 1.8 gather_fusion.2
  81.7 3.5 gather_fusion.3
  85.3 1.8 gather_fusion.4
  87.2 3.5 gather_fusion.5
  90.8 1.8 gather_fusion.6
  92.7 3.5 gather_fusion.7
  96.2 1.8 gather_fusion.8
  98.2 3.5 gather_fusion.9
  103.7 3.5 gather_fusion.11
  107.2 1.8 gather_fusion.12
  109.2 3.5 gather_fusion.13
  114.7 3.5 gather_fusion.15
  123.2 1.9 fusion.81
  125.0 1.9 copy-done.1
  129.1 4.2 fusion.84
  133.4 1.9 fusion.85
  135.5 3.7 fusion.83
  141.4 3.5 gather_fusion.1
  148.9 3.5 gather_fusion.3
  154.3 3.5 gather_fusion.5
  159.8 3.5 gather_fusion.7
  165.3 3.5 gather_fusion.9
  170.8 3.5 gather_fusion.11
  176.3 3.5 gather_fusion.13
  181.8 3.5 gather_fusion.15
  190.3 1.9 fusion.81
  192.1 1.9 copy-done.1
  196.2 4.2 fusion.84
  200.5 1.9 fusion.85
  202.6 3.7 fusion.83
  207.9 71.3 %all-gather.2.cloned.1.call-done = bf16[1024,1024]{1,0:T(8,128)(2,1)} async-done(((bf16[1024,128]{1,0:T(8,128)(2,1)}), bf16[1024,1024]{1,0:T(8,128)(2,1)}) %all-gather.2.cloned.1.call-update) | async-done | bytes 2097168 | tf_op jit(solution)/shard_map/all_gather | solution.py:85
  279.1 5.9 %fusion.51 = f32[1024,1024]{1,0:T(8,128)} fusion(bf16[1024,1024]{1,0:T(8,128)(2,1)} %all-gather.2.cloned.1.call-done, bf16[1024,1024]{1,0:T(8,128)(2,1)S(1)} %copy-done), kind=kOutput, calls=%fused_computation.86 | convolution fusion | flops 2147483648 | bytes 8388608 | tf_op jit(solution)/shard_map/dot_general | solution.py:87
  286.0 11.2 %all_to_all.83 = bf16[8,128,128]{2,1,0:T(8,128)(2,1)S(1)} all-to-all(bf16[8,128,128]{2,1,0:T(8,128)(2,1)S(1)} %bitcast.265), channel_id=1, replica_groups=mesh['dp'=64,'head'=8] {'head'}, dimensions={0} | all-to-all | bytes 524288 | tf_op jit(solution)/shard_map/all_to_all | solution.py:94
  298.3 222.0 %reduce-scatter.2.cloned.1.call-done = f32[16,1024]{1,0:T(8,128)} async-done(((f32[1024,1024]{1,0:T(8,128)}), f32[16,1024]{1,0:T(8,128)}) %reduce-scatter.2.cloned.1.call-update) | async-done | bytes 65552 | tf_op jit(solution)/shard_map/reduce_scatter | solution.py:86
  (140 shorter events, 46.0 us)
Async XLA Ops:
  7.2 271.9 %copy-start = (bf16[1024,1024]{1,0:T(8,128)(2,1)S(1)}, bf16[1024,1024]{1,0:T(8,128)(2,1)}, u32[]{:S(2)}) copy-start(bf16[1024,1024]{1,0:T(8,128)(2,1)} %param.9) | copy-start | bytes 6291460
  9.0 16.8 %all-to-all-start.1 = ((bf16[128,8,128]{2,0,1:T(8,128)(2,1)}), bf16[128,8,128]{2,0,1:T(8,128)(2,1)}, u32[]{:S(2)}, u32[]{:S(2)}) async-start(bf16[128,8,128]{2,0,1:T(8,128)(2,1)} %copy_bitcast_fusion.1), calls=%async_computation.1 | async-start | bytes 524288 | tf_op jit(solution)/shard_map/all_to_all | solution.py:70
  18.7 29.1 %copy-start.5 = (bf16[128,1024]{1,0:T(8,128)(2,1)S(1)}, bf16[128,1024]{1,0:T(8,128)(2,1)}, u32[]{:S(2)}) copy-start(bf16[128,1024]{1,0:T(8,128)(2,1)} %param.12) | copy-start | bytes 786436
  21.0 45.5 %copy-start.9 = (s32[1024]{0:T(1024)S(1)}, s32[1024]{0:T(1024)}, u32[]{:S(2)}) copy-start(s32[1024]{0:T(1024)} %param.14) | copy-start | bytes 12292
  25.8 16.4 %all-to-all-start = ((bf16[128,8,512]{0,2,1:T(8,128)(2,1)}), bf16[128,8,512]{0,2,1:T(8,128)(2,1)S(1)}, u32[]{:S(2)}, u32[]{:S(2)}) async-start(bf16[128,8,512]{0,2,1:T(8,128)(2,1)} %bitcast.260), calls=%async_computation | async-start | bytes 2097152 | tf_op jit(solution)/shard_map/all_to_all | solution.py:68
  33.4 40.2 %copy-start.10 = (s32[2]{0:T(128)S(1)}, s32[2]{0:T(128)}, u32[]{:S(2)}) copy-start(s32[2]{0:T(128)} %param.15) | copy-start | bytes 28
  42.2 19.0 %all-to-all-start.3 = ((bf16[128,8,512]{0,2,1:T(8,128)(2,1)}), bf16[128,8,512]{0,2,1:T(8,128)(2,1)}, u32[]{:S(2)}, u32[]{:S(2)}) async-start(bf16[128,8,512]{0,2,1:T(8,128)(2,1)} %bitcast.261), calls=%async_computation.3 | async-start | bytes 2097152 | tf_op jit(solution)/shard_map/all_to_all | solution.py:69
  61.1 12.4 %all-to-all-start.2 = ((bf16[128,8,128]{2,0,1:T(8,128)(2,1)}), bf16[128,8,128]{2,0,1:T(8,128)(2,1)}, u32[]{:S(2)}, u32[]{:S(2)}) async-start(bf16[128,8,128]{2,0,1:T(8,128)(2,1)} %copy_bitcast_fusion), calls=%async_computation.2 | async-start | bytes 524288 | tf_op jit(solution)/shard_map/all_to_all | solution.py:71
  66.5 212.6 %all-gather.2.cloned.1.call-start = ((), (), s32[]{:S(2)}) async-start(), calls=%async_computation.6 | async-start | bytes 2359296 | tf_op jit(solution)/shard_map/all_gather | solution.py:85
  123.1 4.9 copy-start.4
  125.0 2.0 copy-start.1
  129.1 4.3 copy-start.2
  133.4 2.1 copy-start.3
  135.4 3.8 copy-start.6
  135.4 5.2 copy-start.11
  140.0 0.7 copy-start.7
  190.3 4.9 copy-start.4
  192.1 2.0 copy-start.1
  196.2 4.3 copy-start.2
  200.5 2.1 copy-start.3
  202.5 3.8 copy-start.6
  202.6 5.2 copy-start.11
  207.1 0.7 copy-start.7
  207.8 312.5 %reduce-scatter.2.cloned.1.call-start = ((), (), s32[]{:S(2)}) async-start(), calls=%async_computation.7 | async-start | bytes 4259840 | tf_op jit(solution)/shard_map/reduce_scatter | solution.py:86
  285.0 0.9 copy-start.8
Sparse Core Ops, SparseCore 0:
  207.9 71.1 all-gather.1
  285.2 235.0 reduce-scatter.1
where the time goes:
time: 528 us; the launch traced here: 527 us
  waiting for transfers between devices  322 us (61%)
  local copies, waits for them, and re-layouts  115 us (22%)
  matrix products  29.4 us (6%)
  starting transfers between devices  26.1 us (5%)
  between operations  14.1 us (3%)
  blocking collectives  11.2 us (2%)
  other arithmetic  8.39 us (2%)
    reduce_scatter x1, waiting for transfers between devices, local(): lax.psum_scatter(lax.dot_general(key_all, layer_input, (((0,), (0,)), (()...  222 us
    all_gather x1, waiting for transfers between devices, local(): key_all = lax.all_gather(key_grads, 'head', axis=1, tiled=True)  71.3 us
    gather x16, local copies, waits for them, and re-layouts, ancestry_of(): jumps = jumps[jumps]  55.9 us
    gather x18, local copies, waits for them, and re-layouts, ancestry_of(): reached = reached | reached[jumps]  31.8 us
    all_to_all x1, waiting for transfers between devices, local(): lax.all_to_all(out_grad, 'head', split_axis=1, concat_axis=0, tiled=True)  12.5 us
    all_to_all x1, blocking collectives, local(): lax.all_to_all(value_grads, 'head', split_axis=0, concat_axis=1, tiled=True)  11.2 us
  transfers between devices with their start and end apart: 6, of which 6 were waited for; matrix products, arithmetic and copies ran while one was open for 2% of the time, Pallas kernels for 0%

commit v1 on v0

--- a/solution.py
+++ b/solution.py
@@ -2,6 +2,7 @@
 import jax.numpy as jnp
 from jax import lax
 from jax.sharding import PartitionSpec as P
+from jax.lax import all_to_all, axis_size
 
 HEAD_DIM = 128
 TREE_LEN = 512
@@ -82,7 +83,9 @@
     key_grads, value_grads = lax.map(lambda items: tree_grads(*items), stacked)
     key_grads = key_grads.reshape(trees * TREE_LEN, -1)
     value_grads = value_grads.reshape(trees * TREE_LEN, -1)
-    key_all = lax.all_gather(key_grads, "head", axis=1, tiled=True)
+    key_all = jnp.concatenate(
+        all_to_all(jnp.stack([key_grads] * axis_size("head")), "head", 0, 0), axis=1
+    )
     weight_gradient = lax.psum_scatter(
         lax.dot_general(
             key_all, layer_input, (((0,), (0,)), ((), ())), preferred_element_type=jnp.float32

time: 528 us -> 491 us (0.930)
  waiting for transfers between devices: 322 us -> 255 us
  blocking collectives: 11.2 us -> 41.5 us
    all_gather x1 -> x0, waiting for transfers between devices: 71.3 us -> none  [local(): key_all = lax.all_gather(key_grads, 'head', axis=1, tiled=True)]
    all_to_all x0 -> x1, blocking collectives: none -> 30.2 us  [local(): all_to_all(jnp.stack([key_grads] * axis_size('head')), 'head', 0, 0)]
  transfers between devices with their start and end apart: 6 -> 5, of which waited for: 6 -> 5; matrix products, arithmetic and copies ran while one was open for 2% -> 2% of each run, Pallas kernels for 0% -> 0%
where the time goes in v1:
time: 491 us; the launch traced here: 490 us
  waiting for transfers between devices  255 us (52%)
  local copies, waits for them, and re-layouts  116 us (24%)
  blocking collectives  41.5 us (8%)
  matrix products  27.8 us (6%)
  starting transfers between devices  26 us (5%)
  between operations  14.1 us (3%)
  other arithmetic  8.38 us (2%)
    reduce_scatter x1, waiting for transfers between devices, local(): lax.psum_scatter(lax.dot_general(key_all, layer_input, (((0,), (0,)), (()...  226 us
    gather x16, local copies, waits for them, and re-layouts, ancestry_of(): jumps = jumps[jumps]  55.9 us
    gather x18, local copies, waits for them, and re-layouts, ancestry_of(): reached = reached | reached[jumps]  31.8 us
    all_to_all x1, blocking collectives, local(): all_to_all(jnp.stack([key_grads] * axis_size('head')), 'head', 0, 0)  30.2 us
    all_to_all x1, waiting for transfers between devices, local(): lax.all_to_all(out_grad, 'head', split_axis=1, concat_axis=0, tiled=True)  12.5 us
    all_to_all x1, blocking collectives, local(): lax.all_to_all(value_grads, 'head', split_axis=0, concat_axis=1, tiled=True)  11.3 us
  transfers between devices with their start and end apart: 5, of which 5 were waited for; matrix products, arithmetic and copies ran while one was open for 2% of the time, Pallas kernels for 0%

profile of v1, /device:TPU:8, one launch (start us, length us, event | category | flops | bytes accessed | tf_op | source)
XLA Modules:
  0.0 489.9 jit_solution(13390739025187895570)
XLA Ops:
  7.2 1.8 copy_bitcast_fusion.1
  9.0 9.7 %all-to-all-start.1 = ((bf16[128,8,128]{2,0,1:T(8,128)(2,1)}), bf16[128,8,128]{2,0,1:T(8,128)(2,1)}, u32[]{:S(2)}, u32[]{:S(2)}) async-start(bf16[128,8,128]{2,0,1:T(8,128)(2,1)} %copy_bitcast_fusion.1), calls=%async_computation.1 | async-start | bytes 524288 | tf_op jit(solution)/shard_map/all_to_all | solution.py:71
  18.7 2.3 copy.47
  21.1 4.8 all-to-all-done.1
  25.8 5.3 %all-to-all-start = ((bf16[128,8,512]{0,2,1:T(8,128)(2,1)}), bf16[128,8,512]{0,2,1:T(8,128)(2,1)S(1)}, u32[]{:S(2)}, u32[]{:S(2)}) async-start(bf16[128,8,512]{0,2,1:T(8,128)(2,1)} %bitcast.263), calls=%async_computation | async-start | bytes 2097152 | tf_op jit(solution)/shard_map/all_to_all | solution.py:69
  31.1 2.3 copy.51
  33.4 8.8 %all-to-all-done = bf16[128,8,512]{0,2,1:T(8,128)(2,1)S(1)} async-done(((bf16[128,8,512]{0,2,1:T(8,128)(2,1)}), bf16[128,8,512]{0,2,1:T(8,128)(2,1)S(1)}, u32[]{:S(2)}, u32[]{:S(2)}) %all-to-all-start) | async-done | bytes 1048608 | tf_op jit(solution)/shard_map/all_to_all | solution.py:69
  42.2 5.7 %all-to-all-start.3 = ((bf16[128,8,512]{0,2,1:T(8,128)(2,1)}), bf16[128,8,512]{0,2,1:T(8,128)(2,1)}, u32[]{:S(2)}, u32[]{:S(2)}) async-start(bf16[128,8,512]{0,2,1:T(8,128)(2,1)} %bitcast.264), calls=%async_computation.3 | async-start | bytes 2097152 | tf_op jit(solution)/shard_map/all_to_all | solution.py:70
  48.6 12.5 %all-to-all-done.3 = bf16[128,8,512]{0,2,1:T(8,128)(2,1)} async-done(((bf16[128,8,512]{0,2,1:T(8,128)(2,1)}), bf16[128,8,512]{0,2,1:T(8,128)(2,1)}, u32[]{:S(2)}, u32[]{:S(2)}) %all-to-all-start.3) | async-done | bytes 1048608 | tf_op jit(solution)/shard_map/all_to_all | solution.py:70
  61.1 5.4 %all-to-all-start.2 = ((bf16[128,8,128]{2,0,1:T(8,128)(2,1)}), bf16[128,8,128]{2,0,1:T(8,128)(2,1)}, u32[]{:S(2)}, u32[]{:S(2)}) async-start(bf16[128,8,128]{2,0,1:T(8,128)(2,1)} %copy_bitcast_fusion), calls=%async_computation.2 | async-start | bytes 524288 | tf_op jit(solution)/shard_map/all_to_all | solution.py:72
  68.4 2.3 copy.52
  70.7 2.8 all-to-all-done.2
  73.6 134.4 %while.12 = (s32[]{:T(128)}, bf16[2,512,128]{2,1,0:T(8,128)(2,1)}, bf16[2,512,128]{2,1,0:T(8,128)(2,1)}, bf16[2,512,512]{2,1,0:T(8,128)(2,1)}, s32[2,512]{1,0:T(...) while((s32[]{:T(128)}, bf16[2,512,128]{2,1,0:T(8,128)(2,1)}, ...), condition=%wide.region_4.5_spmd, body=%wide.region_0.4_spmd.sunk | while | flops 1109019648 | bytes 93070192 | solution.py:83
  74.3 3.5 gather_fusion.1
  77.9 1.8 gather_fusion
  81.7 3.5 gather_fusion.3
  87.2 3.5 gather_fusion.5
  92.7 3.5 gather_fusion.7
  98.2 3.5 gather_fusion.9
  101.7 1.8 gather_fusion.10
  103.7 3.5 gather_fusion.11
  109.2 3.5 gather_fusion.13
  112.7 1.8 gather_fusion.14
  114.7 3.5 gather_fusion.15
  118.2 1.8 gather_fusion.16
  123.2 1.9 fusion.81
  125.1 2.0 copy-done.1
  129.2 4.2 fusion.84
  133.4 1.9 fusion.85
  135.5 3.7 fusion.83
  141.4 3.5 gather_fusion.1
  146.9 1.8 gather_fusion.2
  148.9 3.5 gather_fusion.3
  154.4 3.5 gather_fusion.5
  159.9 3.5 gather_fusion.7
  165.4 3.5 gather_fusion.9
  170.9 3.5 gather_fusion.11
  176.3 3.5 gather_fusion.13
  181.8 3.5 gather_fusion.15
  190.4 1.9 fusion.81
  192.2 2.0 copy-done.1
  196.3 4.3 fusion.84
  200.6 1.9 fusion.85
  202.7 3.7 fusion.83
  209.3 30.2 %all_to_all.88 = bf16[8,1024,128]{1,2,0:T(8,128)(2,1)S(1)} all-to-all(bf16[8,1024,128]{1,2,0:T(8,128)(2,1)S(1)} %stack.3), channel_id=1, replica_groups=mesh['dp'=64,'head'=8] {'head'}, dimensions={0} | all-to-all | bytes 4194304 | tf_op jit(solution)/shard_map/all_to_all | solution.py:87
  239.5 4.3 fusion.51
  244.8 11.3 %all_to_all.89 = bf16[8,128,128]{2,1,0:T(8,128)(2,1)S(1)} all-to-all(bf16[8,128,128]{2,1,0:T(8,128)(2,1)S(1)} %bitcast.269), channel_id=1, replica_groups=mesh['dp'=64,'head'=8] {'head'}, dimensions={0} | all-to-all | bytes 524288 | tf_op jit(solution)/shard_map/all_to_all | solution.py:97
  257.1 225.9 %reduce-scatter.2.cloned.1.call-done = f32[16,1024]{1,0:T(8,128)} async-done(((f32[1024,1024]{1,0:T(8,128)}), f32[16,1024]{1,0:T(8,128)}) %reduce-scatter.2.cloned.1.call-update) | async-done | bytes 65552 | tf_op jit(solution)/shard_map/reduce_scatter | solution.py:89
  (140 shorter events, 47.4 us)
Async XLA Ops:
  7.2 232.3 %copy-start = (bf16[1024,1024]{1,0:T(8,128)(2,1)S(1)}, bf16[1024,1024]{1,0:T(8,128)(2,1)}, u32[]{:S(2)}) copy-start(bf16[1024,1024]{1,0:T(8,128)(2,1)} %param.9) | copy-start | bytes 6291460
  9.0 16.8 %all-to-all-start.1 = ((bf16[128,8,128]{2,0,1:T(8,128)(2,1)}), bf16[128,8,128]{2,0,1:T(8,128)(2,1)}, u32[]{:S(2)}, u32[]{:S(2)}) async-start(bf16[128,8,128]{2,0,1:T(8,128)(2,1)} %copy_bitcast_fusion.1), calls=%async_computation.1 | async-start | bytes 524288 | tf_op jit(solution)/shard_map/all_to_all | solution.py:71
  18.7 29.1 %copy-start.5 = (bf16[128,1024]{1,0:T(8,128)(2,1)S(1)}, bf16[128,1024]{1,0:T(8,128)(2,1)}, u32[]{:S(2)}) copy-start(bf16[128,1024]{1,0:T(8,128)(2,1)} %param.12) | copy-start | bytes 786436
  21.1 45.5 %copy-start.9 = (s32[1024]{0:T(1024)S(1)}, s32[1024]{0:T(1024)}, u32[]{:S(2)}) copy-start(s32[1024]{0:T(1024)} %param.14) | copy-start | bytes 12292
  25.8 16.3 %all-to-all-start = ((bf16[128,8,512]{0,2,1:T(8,128)(2,1)}), bf16[128,8,512]{0,2,1:T(8,128)(2,1)S(1)}, u32[]{:S(2)}, u32[]{:S(2)}) async-start(bf16[128,8,512]{0,2,1:T(8,128)(2,1)} %bitcast.263), calls=%async_computation | async-start | bytes 2097152 | tf_op jit(solution)/shard_map/all_to_all | solution.py:69
  33.4 40.2 %copy-start.10 = (s32[2]{0:T(128)S(1)}, s32[2]{0:T(128)}, u32[]{:S(2)}) copy-start(s32[2]{0:T(128)} %param.15) | copy-start | bytes 28
  42.2 19.0 %all-to-all-start.3 = ((bf16[128,8,512]{0,2,1:T(8,128)(2,1)}), bf16[128,8,512]{0,2,1:T(8,128)(2,1)}, u32[]{:S(2)}, u32[]{:S(2)}) async-start(bf16[128,8,512]{0,2,1:T(8,128)(2,1)} %bitcast.264), calls=%async_computation.3 | async-start | bytes 2097152 | tf_op jit(solution)/shard_map/all_to_all | solution.py:70
  61.1 12.4 %all-to-all-start.2 = ((bf16[128,8,128]{2,0,1:T(8,128)(2,1)}), bf16[128,8,128]{2,0,1:T(8,128)(2,1)}, u32[]{:S(2)}, u32[]{:S(2)}) async-start(bf16[128,8,128]{2,0,1:T(8,128)(2,1)} %copy_bitcast_fusion), calls=%async_computation.2 | async-start | bytes 524288 | tf_op jit(solution)/shard_map/all_to_all | solution.py:72
  66.5 416.5 %reduce-scatter.2.cloned.1.call-start = ((), (), s32[]{:S(2)}) async-start(), calls=%async_computation.7 | async-start | bytes 4259840 | tf_op jit(solution)/shard_map/reduce_scatter | solution.py:89
  123.2 4.9 copy-start.4
  125.0 2.0 copy-start.1
  129.2 4.2 copy-start.2
  133.4 2.1 copy-start.3
  135.5 3.8 copy-start.6
  135.5 5.2 %copy-start.11 = (s32[2]{0:T(128)S(1)}, s32[2]{0:T(128)}, u32[]{:S(2)}) copy-start(s32[2]{0:T(128)} %get-tuple-element.220) | copy-start | bytes 28 | tf_op jit(solution)/shard_map/while
  140.0 0.7 copy-start.7
  190.4 4.9 %copy-start.4 = (bf16[2,512,512]{2,1,0:T(8,128)(2,1)S(1)}, bf16[2,512,512]{2,1,0:T(8,128)(2,1)}, u32[]{:S(2)}) copy-start(bf16[2,512,512]{2,1,0:T(8,128)(2,1)} %get-tuple-element.199) | copy-start | bytes 3145732 | tf_op jit(solution)/shard_map/while
  192.2 2.0 copy-start.1
  196.3 4.3 copy-start.2
  200.6 2.1 copy-start.3
  202.7 3.8 copy-start.6
  202.7 5.2 %copy-start.11 = (s32[2]{0:T(128)S(1)}, s32[2]{0:T(128)}, u32[]{:S(2)}) copy-start(s32[2]{0:T(128)} %get-tuple-element.220) | copy-start | bytes 28 | tf_op jit(solution)/shard_map/while
  207.2 0.7 copy-start.7
  243.8 0.9 copy-start.8
Sparse Core Ops, SparseCore 0:
  244.0 239.0 reduce-scatter.1
